TPU v7x, 32 devices: a whole 2x2x4 slice. The times are simulated.
32 devices in a mesh: gx: 8 (over z, x), gy: 4 (over y, core).
Axes of the slice: x: 2, y: 2, z: 4, core: 2. Of those that a mesh axis runs over, the one named last changes fastest.
Arguments:
- e_field: float32 [3, 128, 128, 256], P(None, 'gx', 'gy'), may hold values from -6 to 6
- h_field: float32 [3, 128, 128, 256], P(None, 'gx', 'gy'), may hold values from -6 to 6
- material: int32 [128, 128, 256], P('gx', 'gy'), may hold values from 0 to 7
- eps_table: float32 [8], replicated, may hold values from 1 to 12
- forward_dft: bfloat16 [4, 2, 3, 128, 128, 256], P(None, None, None, 'gx', 'gy'), may hold values from -6 to 6
- phase_step: float32 [4], replicated, may hold values from 0.3 to 2.8
- interp_kernels: float32 [4, 1024, 128], replicated, may hold values from -0.1875 to 0.1875
- kernel_id: int32 [64, 64], P('gx', 'gy'), may hold values from 0 to 3
- owner_map: int32 [64, 64], P('gx', 'gy'), may hold values from 0 to 31, as said below
- slot_map: int32 [64, 64], P('gx', 'gy'), may hold values from 0 to 63
Outputs:
- e_out: float32 [3, 128, 128, 256], P(None, 'gx', 'gy')
- h_out: float32 [3, 128, 128, 256], P(None, 'gx', 'gy')
- design_grad: float32 [2048, 128], P(('gx', 'gy'))
Inputs may be any that keep to these rules, and one draw needn't show every extreme that they name: `owner_map`: the tiles of one device name no owner more than 8 times; in every draw one owner is named exactly 8 times by the tiles of every device.
All inputs are finite; a program needn't handle non-finite values.
Results may differ from a plain program's by a relative error of at most 0.0003.
Values sent between devices are 32-bit elements; how exact they have to be, the bound alone decides.
A program may use at most 64 MiB of HBM per device.

v0:
```python
import jax
import jax.numpy as jnp
from jax import lax
from jax.sharding import PartitionSpec as P

STEPS = 4
SLOTS = 64


COURANT = 0.5


def shifted(value, axis, steps):
    count = lax.axis_size(axis)
    leading, last = (max(0, -steps), min(count, count - steps))
    return lax.ppermute(value, axis, [(source, source + steps) for source in range(leading, last)])


def ahead_diff(field, plane, axis):
    if plane is None:
        shape = list(field.shape)
        shape[axis] = 1
        plane = jnp.zeros(shape, field.dtype)
    else:
        plane = jnp.expand_dims(plane, axis)
    rest = lax.slice_in_dim(field, 1, field.shape[axis], axis=axis)
    return jnp.concatenate([rest, plane], axis=axis) - field


def behind_diff(field, plane, axis):
    if plane is None:
        shape = list(field.shape)
        shape[axis] = 1
        plane = jnp.zeros(shape, field.dtype)
    else:
        plane = jnp.expand_dims(plane, axis)
    rest = lax.slice_in_dim(field, 0, field.shape[axis] - 1, axis=axis)
    return field - jnp.concatenate([plane, rest], axis=axis)


def per_device(
    e_field,
    h_field,
    material,
    eps_table,
    forward_dft,
    phase_step,
    interp_kernels,
    kernel_id,
    owner_map,
    slot_map,
):
    mat_count = eps_table.shape[0]
    marks = (material[None] == jnp.arange(mat_count, dtype=jnp.int32)[:, None, None, None]).astype(
        jnp.float32
    )
    permittivity = jnp.sum(marks * eps_table[:, None, None, None], axis=0)
    scale = COURANT / permittivity
    waves = forward_dft.shape[0]
    fwd_real = forward_dft[:, 0]
    fwd_imag = forward_dft[:, 1]
    cells_x, cells_y, depth = material.shape
    totals = (
        jnp.zeros(material.shape, jnp.float32),
        jnp.zeros((waves,) + e_field.shape, jnp.float32),
        jnp.zeros((waves,) + e_field.shape, jnp.float32),
    )
    elec_x, elec_y, elec_z = (e_field[0], e_field[1], e_field[2])
    magn_x, magn_y, magn_z = (h_field[0], h_field[1], h_field[2])
    for step_index in range(STEPS):
        plane_x = shifted(jnp.stack([elec_y[0], elec_z[0]]), "gx", -1)
        plane_y = shifted(jnp.stack([elec_x[:, 0], elec_z[:, 0]]), "gy", -1)
        magn_x = magn_x - COURANT * (
            ahead_diff(elec_z, plane_y[1], 1) - ahead_diff(elec_y, None, 2)
        )
        magn_y = magn_y - COURANT * (
            ahead_diff(elec_x, None, 2) - ahead_diff(elec_z, plane_x[1], 0)
        )
        magn_z = magn_z - COURANT * (
            ahead_diff(elec_y, plane_x[0], 0) - ahead_diff(elec_x, plane_y[0], 1)
        )
        back_x = shifted(jnp.stack([magn_y[-1], magn_z[-1]]), "gx", 1)
        back_y = shifted(jnp.stack([magn_x[:, -1], magn_z[:, -1]]), "gy", 1)
        elec_x = elec_x + scale * (behind_diff(magn_z, back_y[1], 1) - behind_diff(magn_y, None, 2))
        elec_y = elec_y + scale * (behind_diff(magn_x, None, 2) - behind_diff(magn_z, back_x[1], 0))
        elec_z = elec_z + scale * (
            behind_diff(magn_y, back_x[0], 0) - behind_diff(magn_x, back_y[0], 1)
        )
        elec = jnp.stack([elec_x, elec_y, elec_z])
        accumulate_sens, accumulate_acc_real, accumulate_acc_imag = totals
        moment = float(step_index + 1)
        cosines = jnp.cos(phase_step * moment)
        sine_terms = jnp.sin(phase_step * moment)
        accumulate_acc_real = accumulate_acc_real + cosines[:, None, None, None, None] * elec[None]
        accumulate_acc_imag = (
            accumulate_acc_imag + sine_terms[:, None, None, None, None] * elec[None]
        )
        totals = (accumulate_sens, accumulate_acc_real, accumulate_acc_imag)
    sens, acc_real, acc_imag = totals
    for wave in range(waves):
        sens = sens + jnp.sum(
            fwd_real[wave].astype(jnp.float32) * acc_real[wave]
            - fwd_imag[wave].astype(jnp.float32) * acc_imag[wave],
            axis=0,
        )
    sens = sens / float(waves * STEPS)
    tile_count = cells_x * cells_y // 4
    tile_rows = (
        sens.reshape(cells_x // 2, 2, cells_y // 2, 2, depth)
        .transpose(0, 2, 1, 3, 4)
        .reshape(tile_count, 4 * depth)
    )
    all_kernels = jnp.einsum(
        "tc,kcv->tkv", tile_rows, interp_kernels, precision=lax.Precision.HIGHEST
    )
    kernel_total = interp_kernels.shape[0]
    selector = (
        kernel_id.reshape(-1)[:, None] == jnp.arange(kernel_total, dtype=jnp.int32)[None, :]
    ).astype(jnp.float32)
    restricted = jnp.sum(all_kernels * selector[:, :, None], axis=1)
    voxels = restricted.shape[1]
    owners = owner_map.reshape(-1)
    slot_index = slot_map.reshape(-1)
    size_x = lax.axis_size("gx")
    size_y = lax.axis_size("gy")
    owner_count = size_x * size_y
    capacity = max(2, (2 * tile_count + owner_count - 1) // owner_count)
    order = jnp.arange(tile_count, dtype=jnp.int32)
    earlier = (owners[None, :] == owners[:, None]) & (order[None, :] < order[:, None])
    position = owners * capacity + jnp.sum(earlier.astype(jnp.int32), axis=1)
    placement = (
        position[None, :] == jnp.arange(owner_count * capacity, dtype=jnp.int32)[:, None]
    ).astype(jnp.float32)
    send_values = jnp.dot(placement, restricted, precision=lax.Precision.HIGHEST)
    send_slots = (
        jnp.dot(placement, (slot_index + 1).astype(jnp.float32), precision=lax.Precision.HIGHEST)
        - 1.0
    )
    got_values, got_slots = (
        lax.all_to_all(
            send_values.reshape(owner_count, capacity, voxels),
            ("gx", "gy"),
            split_axis=0,
            concat_axis=0,
            tiled=True,
        ),
        lax.all_to_all(
            send_slots.reshape(owner_count, capacity),
            ("gx", "gy"),
            split_axis=0,
            concat_axis=0,
            tiled=True,
        ),
    )
    got_values = got_values.reshape(owner_count * capacity, voxels)
    got_slots = got_slots.reshape(owner_count * capacity)
    gather_table = (got_slots[None, :] == jnp.arange(SLOTS, dtype=jnp.float32)[:, None]).astype(
        jnp.float32
    )
    design_grad = jnp.dot(gather_table, got_values, precision=lax.Precision.HIGHEST)
    e_out = jnp.stack([elec_x, elec_y, elec_z])
    h_out = jnp.stack([magn_x, magn_y, magn_z])
    return (e_out, h_out, design_grad)


def solution(mesh):
    return jax.shard_map(
        per_device,
        mesh=mesh,
        in_specs=(
            P(None, "gx", "gy", None),
            P(None, "gx", "gy", None),
            P("gx", "gy", None),
            P(),
            P(None, None, None, "gx", "gy", None),
            P(),
            P(),
            P("gx", "gy"),
            P("gx", "gy"),
            P("gx", "gy"),
        ),
        out_specs=(P(None, "gx", "gy", None), P(None, "gx", "gy", None), P(("gx", "gy"), None)),
        check_vma=False,
    )
```

profile of v0, /device:TPU:0, one launch (start us, length us, event | category | flops | bytes accessed | tf_op | source)
XLA Modules:
  0.0 125.7 jit_solution(5972832719198561495)
XLA Ops:
  0.7 2.4 %slice_bitcast_fusion.9 = (f32[16,32,256]{2,1,0:T(8,128)}, f32[16,32,256]{2,1,0:T(8,128)S(1)}, f32[16,32,256]{2,1,0:T(8,128)S(1)}) fusion(f32[3,16,32,256]{3,2,1,0:T(8,128)} %param.10), kind=kLoop, calls=%fused_computation.144 | loop fusion | bytes 3145728 | tf_op jit(solution)/shard_map/squeeze | solution.py:68
  3.2 1.3 %collective-permute-start.1 = (f32[2,16,256]{2,0,1:T(2,128)S(1)}, f32[2,16,256]{2,0,1:T(2,128)S(1)}, u32[]{:S(2)}, u32[]{:S(2)}) collective-permute-start(f32[2,16,256]{2,0,1:T(2,128)S(1)} %pad_maximum_fusion.13), channel_id=1, source_target_pairs={{1,0},{2,1},{3,2},{5,4},{6,5},{7,6},{9,8},{10,9},{11,10},{13,12},{... | collective-permute-start | bytes 98312 | tf_op jit(solution)/shard_map/ppermute | solution.py:16
  4.5 0.8 slice_bitcast_fusion.14
  5.3 1.3 %collective-permute-start = (f32[2,32,256]{2,1,0:T(8,128)S(1)}, f32[2,32,256]{2,1,0:T(8,128)S(1)}, u32[]{:S(2)}, u32[]{:S(2)}) collective-permute-start(f32[2,32,256]{2,1,0:T(8,128)S(1)} %pad_maximum_fusion.5), channel_id=1, source_target_pairs={{4,0},{8,4},{12,8},{16,12},{20,16},{24,20},{28,24},{5,1},{9,5},{13... | collective-permute-start | bytes 196616 | tf_op jit(solution)/shard_map/ppermute | solution.py:16
  7.1 0.8 all_to_all.9
  7.8 9.1 %all-to-all-start = ((f32[32,1,8]{2,1,0:T(1,128)}), f32[32,1,8]{2,1,0:T(1,128)S(1)}, u32[]{:S(2)}, u32[]{:S(2)}) async-start(f32[32,1,8]{2,1,0:T(1,128)} %bitcast.49), calls=%async_computation | async-start | bytes 32768 | tf_op jit(solution)/shard_map/all_to_all | solution.py:147
  16.9 2.2 %slice_bitcast_fusion.12 = (f32[15,32,256]{2,1,0:T(8,128)}, f32[15,32,256]{2,1,0:T(8,128)}) fusion(f32[3,16,32,256]{3,2,1,0:T(8,128)} %param.10), kind=kLoop, calls=%fused_computation.147 | loop fusion | bytes 1966080 | tf_op jit(solution)/shard_map/slice | solution.py:26
  19.3 1.7 %select_reduce_fusion = f32[16,32,256]{2,1,0:T(8,128)S(1)} fusion(f32[8]{0:T(128)S(1)} %copy-done.11, s32[16,32,256]{2,1,0:T(8,128)} %param.12), kind=kLoop, calls=%fused_computation.2 | loop fusion | flops 3014656 | bytes 1048608 | tf_op jit(solution)/shard_map/reduce_sum | solution.py:57
  21.1 0.2 slice.586
  21.4 0.7 copy-done.4
  22.1 0.2 slice.581
  22.4 0.2 copy-done.1
  22.8 0.7 fusion.22
  23.7 2.2 %collective-permute-start.2 = (f32[2,16,256]{2,0,1:T(2,128)S(1)}, f32[2,16,256]{2,0,1:T(2,128)S(1)}, u32[]{:S(2)}, u32[]{:S(2)}) collective-permute-start(f32[2,16,256]{2,0,1:T(2,128)S(1)} %pad_maximum_fusion.14), channel_id=1, source_target_pairs={{0,1},{1,2},{2,3},{4,5},{5,6},{6,7},{8,9},{9,10},{10,11},{12,13},{... | collective-permute-start | bytes 98312 | tf_op jit(solution)/shard_map/ppermute | solution.py:16
  26.0 3.6 %collective-permute-start.3 = (f32[2,32,256]{2,1,0:T(8,128)S(1)}, f32[2,32,256]{2,1,0:T(8,128)S(1)}, u32[]{:S(2)}, u32[]{:S(2)}) collective-permute-start(f32[2,32,256]{2,1,0:T(8,128)S(1)} %pad_maximum_fusion.6), channel_id=1, source_target_pairs={{0,4},{4,8},{8,12},{12,16},{16,20},{20,24},{24,28},{1,5},{5,9},{9,... | collective-permute-start | bytes 196616 | tf_op jit(solution)/shard_map/ppermute | solution.py:16
  29.6 2.0 %collective-permute-done.3 = f32[2,32,256]{2,1,0:T(8,128)S(1)} collective-permute-done((f32[2,32,256]{2,1,0:T(8,128)S(1)}, f32[2,32,256]{2,1,0:T(8,128)S(1)}, u32[]{:S(2)}, u32[]{:S(2)}) %collective-permute-start.3) | collective-permute-done | bytes 65568 | tf_op jit(solution)/shard_map/ppermute | solution.py:16
  31.6 0.9 fusion.25
  32.6 1.3 %collective-permute-start.5 = (f32[2,16,256]{2,0,1:T(2,128)S(1)}, f32[2,16,256]{2,0,1:T(2,128)S(1)}, u32[]{:S(2)}, u32[]{:S(2)}) collective-permute-start(f32[2,16,256]{2,0,1:T(2,128)S(1)} %pad_maximum_fusion.15), channel_id=1, source_target_pairs={{1,0},{2,1},{3,2},{5,4},{6,5},{7,6},{9,8},{10,9},{11,10},{13,12},{... | collective-permute-start | bytes 98312 | tf_op jit(solution)/shard_map/ppermute | solution.py:16
  34.2 0.2 slice.608
  34.4 0.2 slice.613
  34.7 1.3 %collective-permute-start.4 = (f32[2,32,256]{2,1,0:T(8,128)S(1)}, f32[2,32,256]{2,1,0:T(8,128)S(1)}, u32[]{:S(2)}, u32[]{:S(2)}) collective-permute-start(f32[2,32,256]{2,1,0:T(8,128)S(1)} %pad_maximum_fusion.7), channel_id=1, source_target_pairs={{4,0},{8,4},{12,8},{16,12},{20,16},{24,20},{28,24},{5,1},{9,5},{13... | collective-permute-start | bytes 196616 | tf_op jit(solution)/shard_map/ppermute | solution.py:16
  36.1 5.6 %collective-permute-done.4 = f32[2,32,256]{2,1,0:T(8,128)S(1)} collective-permute-done((f32[2,32,256]{2,1,0:T(8,128)S(1)}, f32[2,32,256]{2,1,0:T(8,128)S(1)}, u32[]{:S(2)}, u32[]{:S(2)}) %collective-permute-start.4) | collective-permute-done | bytes 65568 | tf_op jit(solution)/shard_map/ppermute | solution.py:16
  41.7 0.7 fusion.40
  42.5 2.1 %collective-permute-start.6 = (f32[2,16,256]{2,0,1:T(2,128)S(1)}, f32[2,16,256]{2,0,1:T(2,128)S(1)}, u32[]{:S(2)}, u32[]{:S(2)}) collective-permute-start(f32[2,16,256]{2,0,1:T(2,128)S(1)} %pad_maximum_fusion.16), channel_id=1, source_target_pairs={{0,1},{1,2},{2,3},{4,5},{5,6},{6,7},{8,9},{9,10},{10,11},{12,13},{... | collective-permute-start | bytes 98312 | tf_op jit(solution)/shard_map/ppermute | solution.py:16
  44.7 5.0 %collective-permute-start.7 = (f32[2,32,256]{2,1,0:T(8,128)S(1)}, f32[2,32,256]{2,1,0:T(8,128)S(1)}, u32[]{:S(2)}, u32[]{:S(2)}) collective-permute-start(f32[2,32,256]{2,1,0:T(8,128)S(1)} %pad_maximum_fusion.8), channel_id=1, source_target_pairs={{0,4},{4,8},{8,12},{12,16},{16,20},{20,24},{24,28},{1,5},{5,9},{9,... | collective-permute-start | bytes 196616 | tf_op jit(solution)/shard_map/ppermute | solution.py:16
  49.7 1.8 %collective-permute-done.7 = f32[2,32,256]{2,1,0:T(8,128)S(1)} collective-permute-done((f32[2,32,256]{2,1,0:T(8,128)S(1)}, f32[2,32,256]{2,1,0:T(8,128)S(1)}, u32[]{:S(2)}, u32[]{:S(2)}) %collective-permute-start.7) | collective-permute-done | bytes 65568 | tf_op jit(solution)/shard_map/ppermute | solution.py:16
  51.6 0.9 fusion.43
  52.6 1.3 %collective-permute-start.9 = (f32[2,16,256]{2,0,1:T(2,128)S(1)}, f32[2,16,256]{2,0,1:T(2,128)S(1)}, u32[]{:S(2)}, u32[]{:S(2)}) collective-permute-start(f32[2,16,256]{2,0,1:T(2,128)S(1)} %pad_maximum_fusion.17), channel_id=1, source_target_pairs={{1,0},{2,1},{3,2},{5,4},{6,5},{7,6},{9,8},{10,9},{11,10},{13,12},{... | collective-permute-start | bytes 98312 | tf_op jit(solution)/shard_map/ppermute | solution.py:16
  54.2 0.2 slice.636
  54.4 0.2 slice.641
  54.7 1.3 %collective-permute-start.8 = (f32[2,32,256]{2,1,0:T(8,128)S(1)}, f32[2,32,256]{2,1,0:T(8,128)S(1)}, u32[]{:S(2)}, u32[]{:S(2)}) collective-permute-start(f32[2,32,256]{2,1,0:T(8,128)S(1)} %pad_maximum_fusion.9), channel_id=1, source_target_pairs={{4,0},{8,4},{12,8},{16,12},{20,16},{24,20},{28,24},{5,1},{9,5},{13... | collective-permute-start | bytes 196616 | tf_op jit(solution)/shard_map/ppermute | solution.py:16
  56.0 0.3 collective-permute-done.9
  56.3 4.9 %collective-permute-done.8 = f32[2,32,256]{2,1,0:T(8,128)S(1)} collective-permute-done((f32[2,32,256]{2,1,0:T(8,128)S(1)}, f32[2,32,256]{2,1,0:T(8,128)S(1)}, u32[]{:S(2)}, u32[]{:S(2)}) %collective-permute-start.8) | collective-permute-done | bytes 65568 | tf_op jit(solution)/shard_map/ppermute | solution.py:16
  61.2 0.7 fusion.58
  62.0 2.4 %collective-permute-start.10 = (f32[2,16,256]{2,0,1:T(2,128)S(1)}, f32[2,16,256]{2,0,1:T(2,128)S(1)}, u32[]{:S(2)}, u32[]{:S(2)}) collective-permute-start(f32[2,16,256]{2,0,1:T(2,128)S(1)} %pad_maximum_fusion.18), channel_id=1, source_target_pairs={{0,1},{1,2},{2,3},{4,5},{5,6},{6,7},{8,9},{9,10},{10,11},{12,13},{... | collective-permute-start | bytes 98312 | tf_op jit(solution)/shard_map/ppermute | solution.py:16
  64.6 4.8 %collective-permute-start.11 = (f32[2,32,256]{2,1,0:T(8,128)S(1)}, f32[2,32,256]{2,1,0:T(8,128)S(1)}, u32[]{:S(2)}, u32[]{:S(2)}) collective-permute-start(f32[2,32,256]{2,1,0:T(8,128)S(1)} %pad_maximum_fusion.10), channel_id=1, source_target_pairs={{0,4},{4,8},{8,12},{12,16},{16,20},{20,24},{24,28},{1,5},{5,9},{9,... | collective-permute-start | bytes 196616 | tf_op jit(solution)/shard_map/ppermute | solution.py:16
  69.5 1.8 %collective-permute-done.11 = f32[2,32,256]{2,1,0:T(8,128)S(1)} collective-permute-done((f32[2,32,256]{2,1,0:T(8,128)S(1)}, f32[2,32,256]{2,1,0:T(8,128)S(1)}, u32[]{:S(2)}, u32[]{:S(2)}) %collective-permute-start.11) | collective-permute-done | bytes 65568 | tf_op jit(solution)/shard_map/ppermute | solution.py:16
  71.3 0.9 fusion.61
  72.3 1.3 %collective-permute-start.13 = (f32[2,16,256]{2,0,1:T(2,128)S(1)}, f32[2,16,256]{2,0,1:T(2,128)S(1)}, u32[]{:S(2)}, u32[]{:S(2)}) collective-permute-start(f32[2,16,256]{2,0,1:T(2,128)S(1)} %pad_maximum_fusion.19), channel_id=1, source_target_pairs={{1,0},{2,1},{3,2},{5,4},{6,5},{7,6},{9,8},{10,9},{11,10},{13,12},{... | collective-permute-start | bytes 98312 | tf_op jit(solution)/shard_map/ppermute | solution.py:16
  73.9 0.2 slice.664
  74.1 0.2 slice.669
  74.4 1.3 %collective-permute-start.12 = (f32[2,32,256]{2,1,0:T(8,128)S(1)}, f32[2,32,256]{2,1,0:T(8,128)S(1)}, u32[]{:S(2)}, u32[]{:S(2)}) collective-permute-start(f32[2,32,256]{2,1,0:T(8,128)S(1)} %pad_maximum_fusion.11), channel_id=1, source_target_pairs={{4,0},{8,4},{12,8},{16,12},{20,16},{24,20},{28,24},{5,1},{9,5},{13... | collective-permute-start | bytes 196616 | tf_op jit(solution)/shard_map/ppermute | solution.py:16
  75.7 1.0 collective-permute-done.13
  76.7 4.2 %collective-permute-done.12 = f32[2,32,256]{2,1,0:T(8,128)S(1)} collective-permute-done((f32[2,32,256]{2,1,0:T(8,128)S(1)}, f32[2,32,256]{2,1,0:T(8,128)S(1)}, u32[]{:S(2)}, u32[]{:S(2)}) %collective-permute-start.12) | collective-permute-done | bytes 65568 | tf_op jit(solution)/shard_map/ppermute | solution.py:16
  80.9 0.7 fusion.76
  81.7 3.1 %collective-permute-start.14 = (f32[2,16,256]{2,0,1:T(2,128)S(1)}, f32[2,16,256]{2,0,1:T(2,128)S(1)}, u32[]{:S(2)}, u32[]{:S(2)}) collective-permute-start(f32[2,16,256]{2,0,1:T(2,128)S(1)} %pad_maximum_fusion.20), channel_id=1, source_target_pairs={{0,1},{1,2},{2,3},{4,5},{5,6},{6,7},{8,9},{9,10},{10,11},{12,13},{... | collective-permute-start | bytes 98312 | tf_op jit(solution)/shard_map/ppermute | solution.py:16
  85.0 4.7 %collective-permute-start.15 = (f32[2,32,256]{2,1,0:T(8,128)S(1)}, f32[2,32,256]{2,1,0:T(8,128)S(1)}, u32[]{:S(2)}, u32[]{:S(2)}) collective-permute-start(f32[2,32,256]{2,1,0:T(8,128)S(1)} %pad_maximum_fusion.12), channel_id=1, source_target_pairs={{0,4},{4,8},{8,12},{12,16},{16,20},{20,24},{24,28},{1,5},{5,9},{9,... | collective-permute-start | bytes 196616 | tf_op jit(solution)/shard_map/ppermute | solution.py:16
  89.8 1.7 %collective-permute-done.15 = f32[2,32,256]{2,1,0:T(8,128)S(1)} collective-permute-done((f32[2,32,256]{2,1,0:T(8,128)S(1)}, f32[2,32,256]{2,1,0:T(8,128)S(1)}, u32[]{:S(2)}, u32[]{:S(2)}) %collective-permute-start.15) | collective-permute-done | bytes 65568 | tf_op jit(solution)/shard_map/ppermute | solution.py:16
  91.4 0.8 fusion.80
  92.4 3.0 %multiply_add_fusion.1 = (f32[4,3,16,32,256]{4,3,2,1,0:T(8,128)S(1)}, f32[4,3,16,32,256]{4,3,2,1,0:T(8,128)S(1)}) fusion(f32[3,16,32,256]{3,2,1,0:T(8,128)S(1)} %pad_maximum_fusion, f32[4]{0:T(128)S(1)} %get-tuple-element.79, f32[3,16,32,256]{3,2,1,0:T(8,128)S(1)} %pad_maximum_fusion.4, f32[4]{0:T(128)S(1)} %get-tuple-element.76, ...), kind=kLoop, calls=%fused_computation.1 | loop fusion | flops 22020096 | bytes 18874496 | tf_op jit(solution)/shard_map/add | solution.py:94
  95.5 0.3 slice-done.1
  95.8 2.5 %fusion.10 = (f32[16,32,256]{2,1,0:T(8,128)S(1)}, f32[16,32,256]{2,1,0:T(8,128)S(1)}, f32[16,32,256]{2,1,0:T(8,128)S(1)}, f32[16,32,256]{2,1,0:T(8,128)S(1)}) fusion(f32[4,3,16,32,256]{4,3,2,1,0:T(8,128)S(1)} %get-tuple-element.8, f32[4,3,16,32,256]{4,3,2,1,0:T(8,128)S(1)} %get-tuple-element.7, bf16[4,2,3,16,32,256]{5,4,3,2,1,0:T(8,128)(2,1)S(1)} %bitcast.257), kind=kLoop, calls=%fused_computation.19 | loop fusion | flops 8912896 | bytes 20971520 | tf_op jit(solution)/shard_map/reduce_sum | solution.py:101
  98.3 1.0 add_multiply_fusion
  99.3 2.2 %div.14 = f32[8,2,16,2,256]{4,3,2,1,0:T(2,128)} reshape(f32[16,32,256]{2,1,0:T(8,128)} %add_multiply_fusion) | data formatting | bytes 1048576 | tf_op jit(solution)/shard_map/div | solution.py:106
  101.4 2.0 %copy.17 = f32[8,16,2,2,256]{4,3,2,1,0:T(2,128)} copy(f32[8,16,2,2,256]{4,3,1,2,0:T(2,128)} %bitcast.258) | data formatting | bytes 1048576 | tf_op jit(solution)/shard_map/transpose | solution.py:110
  103.5 2.3 %reshape.149 = f32[128,1024,1]{1,0,2:T(8,128)} reshape(f32[8,16,2,2,256]{4,3,2,1,0:T(2,128)} %copy.17) | data formatting | bytes 1048576 | tf_op jit(solution)/shard_map/reshape | solution.py:111
  105.7 2.3 %fusion.16 = f32[128,128]{1,0:T(8,128)S(1)} fusion(f32[128,1024,1]{1,0,2:T(8,128)} %reshape.149, f32[4,1024,128]{2,1,0:T(8,128)S(1)} %copy-done, f32[128,4]{0,1:T(4,128)S(1)} %fusion.103), kind=kOutput, calls=%fused_computation.34 | convolution fusion | flops 805421056 | bytes 2689024 | tf_op jit(solution)/shard_map/tc,kcv->tkv/dot_general | solution.py:113
  108.1 0.9 fusion.94
  109.0 7.7 %all-to-all-start.1 = ((f32[32,8,128]{2,1,0:T(8,128)}), f32[32,8,128]{2,1,0:T(8,128)S(1)}, u32[]{:S(2)}, u32[]{:S(2)}) async-start(f32[32,8,128]{2,1,0:T(8,128)} %fusion.94), calls=%async_computation.1 | async-start | bytes 262144 | tf_op jit(solution)/shard_map/all_to_all | solution.py:140
  116.7 0.5 broadcast.152
  117.2 0.7 reduce.3
  118.0 2.3 %pad_maximum_fusion.1 = f32[3,16,32,256]{3,2,1,0:T(8,128)} fusion(f32[1,16,32,256]{3,2,1,0:T(8,128)S(1)} %bitcast.241, f32[1,16,32,256]{3,2,1,0:T(8,128)} %bitcast.252, f32[1,16,32,256]{3,2,1,0:T(8,128)S(1)} %bitcast.239), kind=kLoop, calls=%fused_computation.29 | loop fusion | flops 786432 | bytes 3145728 | tf_op jit(solution)/shard_map/stack | solution.py:162
  120.3 4.6 %all-to-all-done.1 = f32[32,8,128]{2,1,0:T(8,128)S(1)} async-done(((f32[32,8,128]{2,1,0:T(8,128)}), f32[32,8,128]{2,1,0:T(8,128)S(1)}, u32[]{:S(2)}, u32[]{:S(2)}) %all-to-all-start.1) | async-done | bytes 131104 | tf_op jit(solution)/shard_map/all_to_all | solution.py:140
  124.9 0.8 fusion.92
  (135 shorter events, 3.5 us)
Async XLA Ops:
  0.6 105.1 %copy-start = (f32[4,1024,128]{2,1,0:T(8,128)S(1)}, f32[4,1024,128]{2,1,0:T(8,128)}, u32[]{:S(2)}) copy-start(f32[4,1024,128]{2,1,0:T(8,128)} %param.16) | copy-start | bytes 6291460
  0.6 5.9 %copy-start.8 = (s32[8,16]{1,0:T(8,128)S(1)}, s32[8,16]{1,0:T(8,128)}, u32[]{:S(2)}) copy-start(s32[8,16]{1,0:T(8,128)} %param.18) | copy-start | bytes 1540
  0.7 6.2 %copy-start.10 = (s32[8,16]{1,0:T(8,128)S(1)}, s32[8,16]{1,0:T(8,128)}, u32[]{:S(2)}) copy-start(s32[8,16]{1,0:T(8,128)} %param.19) | copy-start | bytes 1540
  3.1 16.0 %copy-start.12 = (f32[4]{0:T(128)S(1)}, f32[4]{0:T(128)}, u32[]{:S(2)}) copy-start(f32[4]{0:T(128)} %param.15) | copy-start | bytes 52
  3.1 16.1 %copy-start.9 = (s32[8,16]{1,0:T(8,128)S(1)}, s32[8,16]{1,0:T(8,128)}, u32[]{:S(2)}) copy-start(s32[8,16]{1,0:T(8,128)} %param.17) | copy-start | bytes 1540
  3.1 16.2 %copy-start.11 = (f32[8]{0:T(128)S(1)}, f32[8]{0:T(128)}, u32[]{:S(2)}) copy-start(f32[8]{0:T(128)} %param.13) | copy-start | bytes 100
  3.2 19.1 %collective-permute-start.1 = (f32[2,16,256]{2,0,1:T(2,128)S(1)}, f32[2,16,256]{2,0,1:T(2,128)S(1)}, u32[]{:S(2)}, u32[]{:S(2)}) collective-permute-start(f32[2,16,256]{2,0,1:T(2,128)S(1)} %pad_maximum_fusion.13), channel_id=1, source_target_pairs={{1,0},{2,1},{3,2},{5,4},{6,5},{7,6},{9,8},{10,9},{11,10},{13,12},{... | collective-permute-start | bytes 98312 | tf_op jit(solution)/shard_map/ppermute | solution.py:16
  5.3 17.1 %collective-permute-start = (f32[2,32,256]{2,1,0:T(8,128)S(1)}, f32[2,32,256]{2,1,0:T(8,128)S(1)}, u32[]{:S(2)}, u32[]{:S(2)}) collective-permute-start(f32[2,32,256]{2,1,0:T(8,128)S(1)} %pad_maximum_fusion.5), channel_id=1, source_target_pairs={{4,0},{8,4},{12,8},{16,12},{20,16},{24,20},{28,24},{5,1},{9,5},{13... | collective-permute-start | bytes 196616 | tf_op jit(solution)/shard_map/ppermute | solution.py:16
  7.8 101.1 %all-to-all-start = ((f32[32,1,8]{2,1,0:T(1,128)}), f32[32,1,8]{2,1,0:T(1,128)S(1)}, u32[]{:S(2)}, u32[]{:S(2)}) async-start(f32[32,1,8]{2,1,0:T(1,128)} %bitcast.49), calls=%async_computation | async-start | bytes 32768 | tf_op jit(solution)/shard_map/all_to_all | solution.py:147
  19.3 3.0 %copy-start.7 = (f32[3,16,32,256]{3,2,1,0:T(8,128)S(1)}, f32[3,16,32,256]{3,2,1,0:T(8,128)}, u32[]{:S(2)}) copy-start(f32[3,16,32,256]{3,2,1,0:T(8,128)} %param.11) | copy-start | bytes 4718596
  21.0 1.0 copy-start.4
  21.1 1.5 %copy-start.1 = (f32[3,16,32,256]{3,2,1,0:T(8,128)S(1)}, f32[3,16,32,256]{3,2,1,0:T(8,128)}, u32[]{:S(2)}) copy-start(f32[3,16,32,256]{3,2,1,0:T(8,128)} %param.10) | copy-start | bytes 4718596
  21.1 1.6 %copy-start.5 = (f32[15,32,256]{2,1,0:T(8,128)S(1)}, f32[15,32,256]{2,1,0:T(8,128)}, u32[]{:S(2)}) copy-start(f32[15,32,256]{2,1,0:T(8,128)} %get-tuple-element.18) | copy-start | bytes 1474564
  21.1 1.7 %copy-start.6 = (f32[15,32,256]{2,1,0:T(8,128)S(1)}, f32[15,32,256]{2,1,0:T(8,128)}, u32[]{:S(2)}) copy-start(f32[15,32,256]{2,1,0:T(8,128)} %get-tuple-element.19) | copy-start | bytes 1474564
  23.7 5.9 %collective-permute-start.2 = (f32[2,16,256]{2,0,1:T(2,128)S(1)}, f32[2,16,256]{2,0,1:T(2,128)S(1)}, u32[]{:S(2)}, u32[]{:S(2)}) collective-permute-start(f32[2,16,256]{2,0,1:T(2,128)S(1)} %pad_maximum_fusion.14), channel_id=1, source_target_pairs={{0,1},{1,2},{2,3},{4,5},{5,6},{6,7},{8,9},{9,10},{10,11},{12,13},{... | collective-permute-start | bytes 98312 | tf_op jit(solution)/shard_map/ppermute | solution.py:16
  26.0 5.7 %collective-permute-start.3 = (f32[2,32,256]{2,1,0:T(8,128)S(1)}, f32[2,32,256]{2,1,0:T(8,128)S(1)}, u32[]{:S(2)}, u32[]{:S(2)}) collective-permute-start(f32[2,32,256]{2,1,0:T(8,128)S(1)} %pad_maximum_fusion.6), channel_id=1, source_target_pairs={{0,4},{4,8},{8,12},{12,16},{16,20},{20,24},{24,28},{1,5},{5,9},{9,... | collective-permute-start | bytes 196616 | tf_op jit(solution)/shard_map/ppermute | solution.py:16
  32.6 3.4 %collective-permute-start.5 = (f32[2,16,256]{2,0,1:T(2,128)S(1)}, f32[2,16,256]{2,0,1:T(2,128)S(1)}, u32[]{:S(2)}, u32[]{:S(2)}) collective-permute-start(f32[2,16,256]{2,0,1:T(2,128)S(1)} %pad_maximum_fusion.15), channel_id=1, source_target_pairs={{1,0},{2,1},{3,2},{5,4},{6,5},{7,6},{9,8},{10,9},{11,10},{13,12},{... | collective-permute-start | bytes 98312 | tf_op jit(solution)/shard_map/ppermute | solution.py:16
  34.7 7.0 %collective-permute-start.4 = (f32[2,32,256]{2,1,0:T(8,128)S(1)}, f32[2,32,256]{2,1,0:T(8,128)S(1)}, u32[]{:S(2)}, u32[]{:S(2)}) collective-permute-start(f32[2,32,256]{2,1,0:T(8,128)S(1)} %pad_maximum_fusion.7), channel_id=1, source_target_pairs={{4,0},{8,4},{12,8},{16,12},{20,16},{24,20},{28,24},{5,1},{9,5},{13... | collective-permute-start | bytes 196616 | tf_op jit(solution)/shard_map/ppermute | solution.py:16
  42.5 7.2 %collective-permute-start.6 = (f32[2,16,256]{2,0,1:T(2,128)S(1)}, f32[2,16,256]{2,0,1:T(2,128)S(1)}, u32[]{:S(2)}, u32[]{:S(2)}) collective-permute-start(f32[2,16,256]{2,0,1:T(2,128)S(1)} %pad_maximum_fusion.16), channel_id=1, source_target_pairs={{0,1},{1,2},{2,3},{4,5},{5,6},{6,7},{8,9},{9,10},{10,11},{12,13},{... | collective-permute-start | bytes 98312 | tf_op jit(solution)/shard_map/ppermute | solution.py:16
  44.7 6.8 %collective-permute-start.7 = (f32[2,32,256]{2,1,0:T(8,128)S(1)}, f32[2,32,256]{2,1,0:T(8,128)S(1)}, u32[]{:S(2)}, u32[]{:S(2)}) collective-permute-start(f32[2,32,256]{2,1,0:T(8,128)S(1)} %pad_maximum_fusion.8), channel_id=1, source_target_pairs={{0,4},{4,8},{8,12},{12,16},{16,20},{20,24},{24,28},{1,5},{5,9},{9,... | collective-permute-start | bytes 196616 | tf_op jit(solution)/shard_map/ppermute | solution.py:16
  52.6 3.7 %collective-permute-start.9 = (f32[2,16,256]{2,0,1:T(2,128)S(1)}, f32[2,16,256]{2,0,1:T(2,128)S(1)}, u32[]{:S(2)}, u32[]{:S(2)}) collective-permute-start(f32[2,16,256]{2,0,1:T(2,128)S(1)} %pad_maximum_fusion.17), channel_id=1, source_target_pairs={{1,0},{2,1},{3,2},{5,4},{6,5},{7,6},{9,8},{10,9},{11,10},{13,12},{... | collective-permute-start | bytes 98312 | tf_op jit(solution)/shard_map/ppermute | solution.py:16
  54.7 6.5 %collective-permute-start.8 = (f32[2,32,256]{2,1,0:T(8,128)S(1)}, f32[2,32,256]{2,1,0:T(8,128)S(1)}, u32[]{:S(2)}, u32[]{:S(2)}) collective-permute-start(f32[2,32,256]{2,1,0:T(8,128)S(1)} %pad_maximum_fusion.9), channel_id=1, source_target_pairs={{4,0},{8,4},{12,8},{16,12},{20,16},{24,20},{28,24},{5,1},{9,5},{13... | collective-permute-start | bytes 196616 | tf_op jit(solution)/shard_map/ppermute | solution.py:16
  62.0 7.4 %collective-permute-start.10 = (f32[2,16,256]{2,0,1:T(2,128)S(1)}, f32[2,16,256]{2,0,1:T(2,128)S(1)}, u32[]{:S(2)}, u32[]{:S(2)}) collective-permute-start(f32[2,16,256]{2,0,1:T(2,128)S(1)} %pad_maximum_fusion.18), channel_id=1, source_target_pairs={{0,1},{1,2},{2,3},{4,5},{5,6},{6,7},{8,9},{9,10},{10,11},{12,13},{... | collective-permute-start | bytes 98312 | tf_op jit(solution)/shard_map/ppermute | solution.py:16
  64.6 6.7 %collective-permute-start.11 = (f32[2,32,256]{2,1,0:T(8,128)S(1)}, f32[2,32,256]{2,1,0:T(8,128)S(1)}, u32[]{:S(2)}, u32[]{:S(2)}) collective-permute-start(f32[2,32,256]{2,1,0:T(8,128)S(1)} %pad_maximum_fusion.10), channel_id=1, source_target_pairs={{0,4},{4,8},{8,12},{12,16},{16,20},{20,24},{24,28},{1,5},{5,9},{9,... | collective-permute-start | bytes 196616 | tf_op jit(solution)/shard_map/ppermute | solution.py:16
  72.3 4.4 %collective-permute-start.13 = (f32[2,16,256]{2,0,1:T(2,128)S(1)}, f32[2,16,256]{2,0,1:T(2,128)S(1)}, u32[]{:S(2)}, u32[]{:S(2)}) collective-permute-start(f32[2,16,256]{2,0,1:T(2,128)S(1)} %pad_maximum_fusion.19), channel_id=1, source_target_pairs={{1,0},{2,1},{3,2},{5,4},{6,5},{7,6},{9,8},{10,9},{11,10},{13,12},{... | collective-permute-start | bytes 98312 | tf_op jit(solution)/shard_map/ppermute | solution.py:16
  74.4 6.5 %collective-permute-start.12 = (f32[2,32,256]{2,1,0:T(8,128)S(1)}, f32[2,32,256]{2,1,0:T(8,128)S(1)}, u32[]{:S(2)}, u32[]{:S(2)}) collective-permute-start(f32[2,32,256]{2,1,0:T(8,128)S(1)} %pad_maximum_fusion.11), channel_id=1, source_target_pairs={{4,0},{8,4},{12,8},{16,12},{20,16},{24,20},{28,24},{5,1},{9,5},{13... | collective-permute-start | bytes 196616 | tf_op jit(solution)/shard_map/ppermute | solution.py:16
  81.6 10.6 %copy-start.2 = (f32[16,32,256]{2,1,0:T(8,128)}, f32[16,32,256]{2,1,0:T(8,128)S(1)}, u32[]{:S(2)}) copy-start(f32[16,32,256]{2,1,0:T(8,128)S(1)} %get-tuple-element.33) | copy-start | bytes 1572868
  81.7 8.0 %collective-permute-start.14 = (f32[2,16,256]{2,0,1:T(2,128)S(1)}, f32[2,16,256]{2,0,1:T(2,128)S(1)}, u32[]{:S(2)}, u32[]{:S(2)}) collective-permute-start(f32[2,16,256]{2,0,1:T(2,128)S(1)} %pad_maximum_fusion.20), channel_id=1, source_target_pairs={{0,1},{1,2},{2,3},{4,5},{5,6},{6,7},{8,9},{9,10},{10,11},{12,13},{... | collective-permute-start | bytes 98312 | tf_op jit(solution)/shard_map/ppermute | solution.py:16
  85.0 6.4 %collective-permute-start.15 = (f32[2,32,256]{2,1,0:T(8,128)S(1)}, f32[2,32,256]{2,1,0:T(8,128)S(1)}, u32[]{:S(2)}, u32[]{:S(2)}) collective-permute-start(f32[2,32,256]{2,1,0:T(8,128)S(1)} %pad_maximum_fusion.12), channel_id=1, source_target_pairs={{0,4},{4,8},{8,12},{12,16},{16,20},{20,24},{24,28},{1,5},{5,9},{9,... | collective-permute-start | bytes 196616 | tf_op jit(solution)/shard_map/ppermute | solution.py:16
  92.4 3.1 %copy-start.3 = (f32[3,16,32,256]{3,2,1,0:T(8,128)}, f32[3,16,32,256]{3,2,1,0:T(8,128)S(1)}, u32[]{:S(2)}) copy-start(f32[3,16,32,256]{3,2,1,0:T(8,128)S(1)} %pad_maximum_fusion) | copy-start | bytes 4718596
  92.4 3.1 %slice-start = ((s8[6291456]{0:T(1024)(128)(4,1)}), s8[4194304]{0:T(1024)(128)(4,1)S(1)}, s32[]{:S(2)}) async-start(s8[6291456]{0:T(1024)(128)(4,1)} %bitcast.256), calls=%async_computation.2 | async-start | bytes 8388608
  92.4 3.4 %slice-start.1 = ((s8[6291456]{0:T(1024)(128)(4,1)}), s8[2097152]{0:T(1024)(128)(4,1)S(1)}, s32[]{:S(2)}) async-start(s8[6291456]{0:T(1024)(128)(4,1)} %bitcast.256), calls=%async_computation.3 | async-start | bytes 4194304
  109.0 15.9 %all-to-all-start.1 = ((f32[32,8,128]{2,1,0:T(8,128)}), f32[32,8,128]{2,1,0:T(8,128)S(1)}, u32[]{:S(2)}, u32[]{:S(2)}) async-start(f32[32,8,128]{2,1,0:T(8,128)} %fusion.94), calls=%async_computation.1 | async-start | bytes 262144 | tf_op jit(solution)/shard_map/all_to_all | solution.py:140
where the time goes:
time: 127 us; the launch traced here: 126 us
  starting transfers between devices  55 us (43%)
  waiting for transfers between devices  28 us (22%)
  other arithmetic  18.8 us (15%)
  local copies, waits for them, and re-layouts  18.1 us (14%)
  matrix products  4.17 us (3%)
  between operations  1.74 us (1%)
    ppermute x16, starting transfers between devices, shifted(): lax.ppermute(value, axis, [(source, source + steps) for source in range(l...  38.2 us
    ppermute x16, waiting for transfers between devices, shifted(): lax.ppermute(value, axis, [(source, source + steps) for source in range(l...  23.4 us
    all_to_all x1, starting transfers between devices, per_device(): lax.all_to_all(send_slots.reshape(owner_count, capacity), ('gx', 'gy'), s...  9.08 us
    all_to_all x1, starting transfers between devices, per_device(): lax.all_to_all(send_values.reshape(owner_count, capacity, voxels), ('gx',...  7.7 us
    all_to_all x1, waiting for transfers between devices, per_device(): lax.all_to_all(send_values.reshape(owner_count, capacity, voxels), ('gx',...  4.61 us
    slice x23, local copies, waits for them, and re-layouts, ahead_diff(): rest = lax.slice_in_dim(field, 1, field.shape[axis], axis=axis)  4.39 us
    add x1, other arithmetic, per_device(): accumulate_acc_real + cosines[:, None, None, None, None] * elec[None]  3.03 us
    sub x4, other arithmetic, per_device(): magn_x - COURANT * (ahead_diff(elec_z, plane_y[1], 1) - ahead_diff(elec_y...  2.93 us
  transfers between devices with their start and end apart: 18, of which 10 were waited for; matrix products, arithmetic and copies ran while one was open for 28% of the time, Pallas kernels for 0%

commit v1 on v0

v1 whole, which is shorter than its diff:
```python
import functools

import jax
import jax.numpy as jnp
from jax import lax
from jax.experimental import pallas as pl
from jax.experimental.pallas import tpu as pltpu
from jax.sharding import PartitionSpec as P

STEPS = 4
SLOTS = 64
COURANT = 0.5

F32 = jnp.float32
BF16 = jnp.bfloat16
MESH = pl.DeviceIdType.MESH


def split2(value):
    high = value.astype(BF16)
    return high, (value - high.astype(F32)).astype(BF16)


def dot(lhs, rhs):
    return jnp.dot(lhs, rhs, preferred_element_type=F32)


def dot_rows(lhs, rhs):
    return lax.dot_general(lhs, rhs, (((0,), (0,)), ((), ())), preferred_element_type=F32)


def iota(shape, dim):
    return lax.broadcasted_iota(jnp.int32, shape, dim)


def kernel(
    size_x,
    size_y,
    capacity,
    eps_ref,
    phase_ref,
    e_in,
    h_in,
    mat_in,
    dft_in,
    kern_in,
    kid_in,
    owner_in,
    slot_in,
    e_out,
    h_out,
    grad_ref,
    elec,
    magn,
    mat,
    scale,
    dft,
    kern,
    kern_high,
    kern_low,
    kid,
    owner,
    slot,
    weights,
    sens,
    halo_x,
    halo_y,
    pack_y,
    put,
    got,
    put_slot,
    got_slot,
    in_sem,
    out_sem,
    send_x,
    recv_x,
    send_y,
    recv_y,
    a2a_sem,
):
    count = size_x * size_y
    cells_x, cells_y, depth = mat.shape
    waves = dft.shape[0]
    tile_x, tile_y = kid.shape
    tiles = tile_x * tile_y
    kernels, tile_cells, voxels = kern.shape
    gx = lax.axis_index("gx")
    gy = lax.axis_index("gy")
    me = gx * size_y + gy

    loads = [
        pltpu.make_async_copy(source, target, in_sem.at[place])
        for place, (source, target) in enumerate(
            [
                (e_in, elec),
                (h_in, magn),
                (mat_in, mat),
                (kid_in, kid),
                (owner_in, owner),
                (slot_in, slot),
                (kern_in, kern),
                (dft_in, dft),
            ]
        )
    ]
    for load in loads:
        load.start()

    barrier = pltpu.get_barrier_semaphore()

    def greet(step, carry):
        peer = lax.rem(me + step, count)
        pl.semaphore_signal(
            barrier,
            inc=1,
            device_id=(peer // size_y, lax.rem(peer, size_y)),
            device_id_type=MESH,
        )
        return carry

    lax.fori_loop(1, count, greet, 0)

    row_y = iota((cells_y, depth), 0)
    col_z = iota((cells_y, depth), 1)

    def y_up(v):
        return jnp.where(row_y == cells_y - 1, 0.0, pltpu.roll(v, cells_y - 1, 0))

    def z_up(v):
        return jnp.where(col_z == depth - 1, 0.0, pltpu.roll(v, depth - 1, 1))

    def y_down(v):
        return jnp.where(row_y == 0, 0.0, pltpu.roll(v, 1, 0))

    def z_down(v):
        return jnp.where(col_z == 0, 0.0, pltpu.roll(v, 1, 1))

    def h_plane(x, last):
        ex, ey, ez = elec[0, x], elec[1, x], elec[2, x]
        dx_ey = -ey if last else elec[1, x + 1] - ey
        dx_ez = -ez if last else elec[2, x + 1] - ez
        magn[0, x] = magn[0, x] - COURANT * ((y_up(ez) - ez) - (z_up(ey) - ey))
        magn[1, x] = magn[1, x] - COURANT * ((z_up(ex) - ex) - dx_ez)
        magn[2, x] = magn[2, x] - COURANT * (dx_ey - (y_up(ex) - ex))

    def e_plane(x, first):
        hx, hy, hz = magn[0, x], magn[1, x], magn[2, x]
        dx_hy = hy if first else hy - magn[1, x - 1]
        dx_hz = hz if first else hz - magn[2, x - 1]
        factor = scale[x]
        elec[0, x] = elec[0, x] + factor * ((hz - y_down(hz)) - (hy - z_down(hy)))
        elec[1, x] = elec[1, x] + factor * ((hx - z_down(hx)) - dx_hz)
        elec[2, x] = elec[2, x] + factor * (dx_hy - (hx - y_down(hx)))

    def loop(low, high, body):
        def run(x, carry):
            body(x)
            return carry

        lax.fori_loop(low, high, run, 0)

    def h_interior():
        loop(0, cells_x - 1, lambda x: h_plane(x, False))
        h_plane(cells_x - 1, True)

    def e_interior():
        e_plane(0, True)
        loop(1, cells_x, lambda x: e_plane(x, False))

    def x_copy(half, source, shift):
        return pltpu.make_async_remote_copy(
            src_ref=source,
            dst_ref=halo_x.at[half],
            send_sem=send_x.at[half],
            recv_sem=recv_x.at[half],
            device_id=(gx + shift, gy),
            device_id_type=MESH,
        )

    def y_copy(half, shift):
        return pltpu.make_async_remote_copy(
            src_ref=pack_y.at[half],
            dst_ref=halo_y.at[half],
            send_sem=send_y.at[half],
            recv_sem=recv_y.at[half],
            device_id=(gx, gy + shift),
            device_id_type=MESH,
        )

    has_before_x, has_after_x = gx > 0, gx < size_x - 1
    has_before_y, has_after_y = gy > 0, gy < size_y - 1

    def copies(half):
        if half % 2 == 0:
            return (
                (has_before_x, has_after_x, x_copy(half, elec.at[pl.ds(1, 2), 0], -1)),
                (has_before_y, has_after_y, y_copy(half, -1)),
            )
        return (
            (has_after_x, has_before_x, x_copy(half, magn.at[pl.ds(1, 2), cells_x - 1], 1)),
            (has_after_y, has_before_y, y_copy(half, 1)),
        )

    def send(half):
        (to_x, _, over_x), (to_y, _, over_y) = copies(half)

        @pl.when(to_x)
        def _():
            over_x.start()

        field, row = (elec, 0) if half % 2 == 0 else (magn, cells_y - 1)
        pack_y[half, 0] = field[0, :, pl.ds(row, 1), :]
        pack_y[half, 1] = field[2, :, pl.ds(row, 1), :]

        @pl.when(to_y)
        def _():
            over_y.start()

    def receive(half):
        (to_x, from_x, over_x), (to_y, from_y, over_y) = copies(half)

        @pl.when(from_y)
        def _():
            over_y.wait_recv()
            if half % 2 == 0:
                row = pl.ds(cells_y - 1, 1)
                magn[0, :, row, :] = magn[0, :, row, :] - COURANT * halo_y[half, 1]
                magn[2, :, row, :] = magn[2, :, row, :] + COURANT * halo_y[half, 0]
            else:
                row = pl.ds(0, 1)
                factor = scale[:, row, :]
                elec[0, :, row, :] = elec[0, :, row, :] - factor * halo_y[half, 1]
                elec[2, :, row, :] = elec[2, :, row, :] + factor * halo_y[half, 0]

        @pl.when(from_x)
        def _():
            over_x.wait_recv()
            if half % 2 == 0:
                last = cells_x - 1
                magn[1, last] = magn[1, last] + COURANT * halo_x[half, 1]
                magn[2, last] = magn[2, last] - COURANT * halo_x[half, 0]
            else:
                factor = scale[0]
                elec[1, 0] = elec[1, 0] + factor * halo_x[half, 1]
                elec[2, 0] = elec[2, 0] - factor * halo_x[half, 0]

        @pl.when(to_x)
        def _():
            over_x.wait_send()

        @pl.when(to_y)
        def _():
            over_y.wait_send()

    def make_scale():
        def plane(x):
            kind = mat[x]
            eps = jnp.full(kind.shape, eps_ref[0], F32)
            for index in range(1, eps_ref.shape[0]):
                eps = jnp.where(kind == index, eps_ref[index], eps)
            scale[x] = COURANT / eps

        loop(0, cells_x, plane)

    def make_coefs():
        width = 2 * waves * cells_y
        column = iota((8, width), 1)
        wave = column // (2 * cells_y)
        phase = jnp.full((8, width), phase_ref[0], F32)
        for index in range(1, waves):
            phase = jnp.where(wave == index, phase_ref[index], phase)
        angle = phase * (iota((8, width), 0) + 1).astype(F32)
        imaginary = lax.rem(column // cells_y, 2) == 1
        values = jnp.where(imaginary, -jnp.sin(angle), jnp.cos(angle)) / float(waves * STEPS)
        own = iota((cells_y, width), 0) == lax.rem(iota((cells_y, width), 1), cells_y)
        table = jnp.concatenate(
            [jnp.where(own, values[step : step + 1], 0.0) for step in range(STEPS)], axis=0
        )
        return jnp.concatenate(split2(table), axis=0)

    def make_weights(low, high):
        coefs = make_coefs()
        half = STEPS * cells_y

        def plane(index):
            comp, x = index // cells_x, lax.rem(index, cells_x)
            block = dft[:, :, comp, x].reshape(2 * waves * cells_y, depth)
            both = dot(coefs, block)
            weights[:, comp, x] = (both[:half] + both[half:]).reshape(STEPS, cells_y, depth)

        loop(low * cells_x, high * cells_x, plane)

    def add_sens(step):
        def plane(x):
            total = elec[0, x] * weights[step, 0, x]
            total = total + elec[1, x] * weights[step, 1, x]
            total = total + elec[2, x] * weights[step, 2, x]
            for block in range(depth // 128):
                lanes = total[:, block * 128 : (block + 1) * 128]
                sens[block, x] = lanes if step == 0 else sens[block, x] + lanes

        loop(0, cells_x, plane)

    def as_column(values):
        pick = (iota((tiles, tile_x), 0) // tile_y == iota((tiles, tile_x), 1)).astype(BF16)
        spread = dot(pick, values.astype(F32).astype(BF16))
        keep = iota((tiles, tile_y), 1) == lax.rem(iota((tiles, tile_y), 0), tile_y)
        return jnp.sum(jnp.where(keep, spread, 0.0), axis=1, keepdims=True)

    def as_row(values):
        rows, lanes = values.shape
        size = rows * lanes
        pick = (iota((rows, size), 1) // lanes == iota((rows, size), 0)).astype(BF16)
        spread = dot_rows(values.astype(F32).astype(BF16), pick)
        keep = iota((lanes, size), 0) == lax.rem(iota((lanes, size), 1), lanes)
        return jnp.sum(jnp.where(keep, spread, 0.0), axis=0, keepdims=True)

    def positions():
        own_row = as_row(owner[...])
        own_column = as_column(owner[...])
        earlier = (own_column == own_row) & (iota((tiles, tiles), 0) < iota((tiles, tiles), 1))
        rank = jnp.sum(jnp.where(earlier, 1.0, 0.0), axis=0, keepdims=True)
        return own_row, own_column, rank

    def send_slots():
        own_row, _, rank = positions()
        mine = (iota((count, tiles), 0).astype(F32) == own_row).astype(BF16)
        place = (iota((128, tiles), 0).astype(F32) == rank).astype(F32)
        labels = (place * (as_row(slot[...]) + 1.0)).astype(BF16)
        table = (
            lax.dot_general(mine, labels, (((1,), (1,)), ((), ())), preferred_element_type=F32)
            - 1.0
        )
        put_slot[...] = table.reshape(count, 1, 128)
        got_slot[me] = put_slot[me]

        def push(step, carry):
            peer = lax.rem(me + step, count)
            pltpu.make_async_remote_copy(
                src_ref=put_slot.at[peer],
                dst_ref=got_slot.at[me],
                send_sem=a2a_sem.at[0],
                recv_sem=a2a_sem.at[1],
                device_id=(peer // size_y, lax.rem(peer, size_y)),
                device_id_type=MESH,
            ).start()
            return carry

        lax.fori_loop(1, count, push, 0)

    def wait_all(buffer, place):
        part = buffer.at[pl.ds(0, count - 1)]
        pltpu.make_async_copy(part, part, a2a_sem.at[place]).wait()

    def make_kernels():
        for index in range(kernels):
            high, low = split2(kern[index])
            kern_high[:, index * voxels : (index + 1) * voxels] = high
            kern_low[:, index * voxels : (index + 1) * voxels] = low

    loads[0].wait()
    pl.semaphore_wait(barrier, count - 1)
    send(0)
    loads[1].wait()
    h_interior()
    loads[2].wait()
    make_scale()
    receive(0)
    send(1)
    e_interior()
    loads[7].wait()
    make_weights(0, 2)
    receive(1)
    send(2)
    h_interior()
    make_weights(2, 3)
    add_sens(0)
    receive(2)
    send(3)
    e_interior()
    for place in (3, 4, 5):
        loads[place].wait()
    send_slots()
    receive(3)
    send(4)
    h_interior()
    add_sens(1)
    receive(4)
    send(5)
    e_interior()
    loads[6].wait()
    make_kernels()
    receive(5)
    send(6)
    h_interior()
    add_sens(2)
    receive(6)
    send(7)
    store_h = pltpu.make_async_copy(magn, h_out, out_sem.at[0])
    store_h.start()
    e_interior()
    wait_all(put_slot, 0)
    wait_all(got_slot, 1)
    receive(7)
    store_e = pltpu.make_async_copy(elec, e_out, out_sem.at[1])
    store_e.start()
    add_sens(3)

    total = jnp.zeros((tiles, kernels * voxels), F32)
    for a in range(2):
        for b in range(2):
            part = [
                sens[block, pl.ds(a, cells_x // 2, 2), pl.ds(b, cells_y // 2, 2), :]
                for block in range(depth // 128)
            ]
            part = jnp.concatenate([lanes.reshape(tiles, 128) for lanes in part], axis=1)
            high, low = split2(part)
            rows = slice((2 * a + b) * depth, (2 * a + b + 1) * depth)
            big, small = kern_high[rows, :], kern_low[rows, :]
            total = total + dot(high, big) + (dot(low, big) + dot(high, small))
    kinds = as_column(kid[...])
    restricted = jnp.zeros((tiles, voxels), F32)
    for index in range(kernels):
        restricted = restricted + jnp.where(
            kinds == float(index), total[:, index * voxels : (index + 1) * voxels], 0.0
        )

    own_row, _, rank = positions()
    position = own_row * float(capacity) + rank
    placement = (iota((count * capacity, tiles), 0).astype(F32) == position).astype(BF16)
    high, low = split2(restricted)
    put[...] = (dot(placement, high) + dot(placement, low)).reshape(count, capacity, voxels)
    got[me] = put[me]

    def push(step, carry):
        peer = lax.rem(me + step, count)
        pltpu.make_async_remote_copy(
            src_ref=put.at[peer],
            dst_ref=got.at[me],
            send_sem=a2a_sem.at[2],
            recv_sem=a2a_sem.at[3],
            device_id=(peer // size_y, lax.rem(peer, size_y)),
            device_id_type=MESH,
        ).start()
        return carry

    lax.fori_loop(1, count, push, 0)
    received = got_slot[...].reshape(count, 128)[:, :capacity]
    gather = (
        iota((SLOTS, count * capacity), 0).astype(F32) == as_row(received)
    ).astype(BF16)
    wait_all(got, 3)
    high, low = split2(got[...].reshape(count * capacity, voxels))
    grad_ref[...] = dot(gather, high) + dot(gather, low)
    wait_all(put, 2)
    store_h.wait()
    store_e.wait()


def per_device(
    size_x,
    size_y,
    e_field,
    h_field,
    material,
    eps_table,
    forward_dft,
    phase_step,
    interp_kernels,
    kernel_id,
    owner_map,
    slot_map,
):
    count = size_x * size_y
    cells_x, cells_y, depth = material.shape
    kernels, tile_cells, voxels = interp_kernels.shape
    tiles = cells_x * cells_y // 4
    capacity = max(2, (2 * tiles + count - 1) // count)
    field = jax.ShapeDtypeStruct(e_field.shape, F32)
    anywhere = pl.BlockSpec(memory_space=pl.ANY)
    halves = 2 * STEPS
    return pl.pallas_call(
        functools.partial(kernel, size_x, size_y, capacity),
        out_shape=(field, field, jax.ShapeDtypeStruct((SLOTS, voxels), F32)),
        in_specs=[pl.BlockSpec(memory_space=pltpu.SMEM)] * 2 + [anywhere] * 8,
        out_specs=(anywhere, anywhere, pl.BlockSpec(memory_space=pltpu.VMEM)),
        scratch_shapes=[
            pltpu.VMEM(e_field.shape, F32),
            pltpu.VMEM(h_field.shape, F32),
            pltpu.VMEM(material.shape, jnp.int32),
            pltpu.VMEM(material.shape, F32),
            pltpu.VMEM(forward_dft.shape, BF16),
            pltpu.VMEM(interp_kernels.shape, F32),
            pltpu.VMEM((tile_cells, kernels * voxels), BF16),
            pltpu.VMEM((tile_cells, kernels * voxels), BF16),
            pltpu.VMEM(kernel_id.shape, jnp.int32),
            pltpu.VMEM(owner_map.shape, jnp.int32),
            pltpu.VMEM(slot_map.shape, jnp.int32),
            pltpu.VMEM((STEPS,) + e_field.shape, F32),
            pltpu.VMEM((depth // 128, cells_x, cells_y, 128), F32),
            pltpu.VMEM((halves, 2, cells_y, depth), F32),
            pltpu.VMEM((halves, 2, cells_x, 1, depth), F32),
            pltpu.VMEM((halves, 2, cells_x, 1, depth), F32),
            pltpu.VMEM((count, capacity, voxels), F32),
            pltpu.VMEM((count, capacity, voxels), F32),
            pltpu.VMEM((count, 1, 128), F32),
            pltpu.VMEM((count, 1, 128), F32),
            pltpu.SemaphoreType.DMA((8,)),
            pltpu.SemaphoreType.DMA((2,)),
            pltpu.SemaphoreType.DMA((halves,)),
            pltpu.SemaphoreType.DMA((halves,)),
            pltpu.SemaphoreType.DMA((halves,)),
            pltpu.SemaphoreType.DMA((halves,)),
            pltpu.SemaphoreType.DMA((4,)),
        ],
        compiler_params=pltpu.CompilerParams(
            collective_id=0, has_side_effects=True, vmem_limit_bytes=60 * 2**20
        ),
    )(
        eps_table,
        phase_step,
        e_field,
        h_field,
        material,
        forward_dft,
        interp_kernels,
        kernel_id,
        owner_map,
        slot_map,
    )


def solution(mesh):
    return jax.shard_map(
        functools.partial(per_device, mesh.shape["gx"], mesh.shape["gy"]),
        mesh=mesh,
        in_specs=(
            P(None, "gx", "gy", None),
            P(None, "gx", "gy", None),
            P("gx", "gy", None),
            P(),
            P(None, None, None, "gx", "gy", None),
            P(),
            P(),
            P("gx", "gy"),
            P("gx", "gy"),
            P("gx", "gy"),
        ),
        out_specs=(P(None, "gx", "gy", None), P(None, "gx", "gy", None), P(("gx", "gy"), None)),
        check_vma=False,
    )
```

time: 127 us -> 54.2 us (0.43)
  starting transfers between devices: 55 us -> 0 us
  Pallas kernels: 0 us -> 48.7 us
  waiting for transfers between devices: 28 us -> 0 us
  other arithmetic: 18.8 us -> 0 us
  local copies, waits for them, and re-layouts: 18.1 us -> 4.61 us
  matrix products: 4.17 us -> 0 us
    pallas_call x0 -> x1, Pallas kernels: none -> 48.7 us  [per_device(): pl.pallas_call(functools.partial(kernel, size_x, size_y, capacity), out_s...]
    ppermute x16 -> x0, starting transfers between devices: 38.2 us -> none  [shifted(): lax.ppermute(value, axis, [(source, source + steps) for source in range(l...]
    ppermute x16 -> x0, waiting for transfers between devices: 23.4 us -> none  [shifted(): lax.ppermute(value, axis, [(source, source + steps) for source in range(l...]
    all_to_all x2 -> x0, starting transfers between devices: 16.8 us -> none  [the longest x1 9.08 us: per_device(): lax.all_to_all(send_slots.reshape(owner_count, capacity), ('gx', 'gy'), s...]
    add x5 -> x0, other arithmetic: 5.65 us -> none  [the longest x1 3.03 us: per_device(): accumulate_acc_real + cosines[:, None, None, None, None] * elec[None]]
    slice x54 -> x0, local copies, waits for them, and re-layouts: 5.58 us -> none  [the longest x23 4.39 us: ahead_diff(): rest = lax.slice_in_dim(field, 1, field.shape[axis], axis=axis)]
    all_to_all x2 -> x0, waiting for transfers between devices: 4.62 us -> none  [the longest x1 4.61 us: per_device(): lax.all_to_all(send_values.reshape(owner_count, capacity, voxels), ('gx',...]
    reduce_sum x3 -> x0, other arithmetic: 4.36 us -> none  [the longest x1 2.5 us: per_device(): jnp.sum(fwd_real[wave].astype(jnp.float32) * acc_real[wave] - fwd_imag[wa...]
  transfers between devices with their start and end apart: 18 -> 0, of which waited for: 10 -> 0; matrix products, arithmetic and copies ran while one was open for 28% -> 0% of each run, Pallas kernels for 0% -> 0%
where the time goes in v1:
time: 54.2 us; the launch traced here: 54 us
  Pallas kernels  48.7 us (90%)
  local copies, waits for them, and re-layouts  4.61 us (9%)
  between operations  0.65 us (1%)
    pallas_call x1, Pallas kernels, per_device(): pl.pallas_call(functools.partial(kernel, size_x, size_y, capacity), out_s...  48.7 us
    unnamed x7, local copies, waits for them, and re-layouts  4.61 us

profile of v1, /device:TPU:0, one launch (start us, length us, event | category | flops | bytes accessed | tf_op | source)
XLA Modules:
  0.0 54.0 jit_solution(7622532442193974714)
XLA Ops:
  0.6 48.7 %shard_map.121 = (f32[3,16,32,256]{3,2,1,0:T(8,128)}, f32[3,16,32,256]{3,2,1,0:T(8,128)}, f32[64,128]{1,0:T(8,128)}) custom-call(f32[8]{0:T(128)} %eps_ref.1, f32[4]{0:T(128)} %phase_ref.1, f32[3,16,32,256]{3,2,1,0:T(8,128)} %e_in.1, f32[3,16,32,256]{3,2,1,0:T(8,128)} %h_in.1, s32[16,32,256]{2,1,0:T(8,128)} %mat_in.1, ...), custom_call_target="tpu_custom_call" | custom-call | tf_op jit(solution)/shard_map/pallas_call | solution.py:482
  49.4 0.0 copy-start
  49.4 2.8 %copy.16 = f32[3,16,32,256]{3,2,1,0:T(8,128)} copy(f32[3,16,32,256]{3,2,1,0:T(8,128)} %get-tuple-element.6) | data formatting | bytes 3145728
  52.2 0.0 copy-done
  52.2 0.0 copy-start.1
  52.2 1.1 %copy.17 = f32[3,16,32,256]{3,2,1,0:T(8,128)} copy(f32[3,16,32,256]{3,2,1,0:T(8,128)S(1)} %copy-done) | data formatting | bytes 3145728
  53.4 0.0 copy-done.1
  53.4 0.6 %copy.18 = f32[64,128]{1,0:T(8,128)} copy(f32[64,128]{1,0:T(8,128)S(1)} %copy-done.1) | data formatting | bytes 65536
Async XLA Ops:
  49.4 2.9 %copy-start = (f32[3,16,32,256]{3,2,1,0:T(8,128)S(1)}, f32[3,16,32,256]{3,2,1,0:T(8,128)}, u32[]{:S(2)}) copy-start(f32[3,16,32,256]{3,2,1,0:T(8,128)} %get-tuple-element.7) | copy-start | bytes 4718596
  52.2 1.1 %copy-start.1 = (f32[64,128]{1,0:T(8,128)S(1)}, f32[64,128]{1,0:T(8,128)}, u32[]{:S(2)}) copy-start(f32[64,128]{1,0:T(8,128)} %get-tuple-element.8) | copy-start | bytes 98308

commit v2 on v1

--- a/solution.py
+++ b/solution.py
@@ -10,6 +10,7 @@
 STEPS = 4
 SLOTS = 64
 COURANT = 0.5
+UNROLL = 4
 
 F32 = jnp.float32
 BF16 = jnp.bfloat16
@@ -31,6 +32,15 @@
 
 def iota(shape, dim):
     return lax.broadcasted_iota(jnp.int32, shape, dim)
+
+
+def as_row(values):
+    rows, lanes = values.shape
+    size = rows * lanes
+    pick = (iota((rows, size), 1) // lanes == iota((rows, size), 0)).astype(BF16)
+    spread = dot_rows(values.astype(F32).astype(BF16), pick)
+    keep = iota((lanes, size), 0) == lax.rem(iota((lanes, size), 1), lanes)
+    return jnp.sum(jnp.where(keep, spread, 0.0), axis=0, keepdims=True)
 
 
 def kernel(
@@ -47,11 +57,11 @@
     kid_in,
     owner_in,
     slot_in,
-    e_out,
-    h_out,
-    grad_ref,
-    elec,
+    last_elec,
     magn,
+    put_out,
+    slot_out,
+    elec_steps,
     mat,
     scale,
     dft,
@@ -61,17 +71,15 @@
     kid,
     owner,
     slot,
+    coefs,
     weights,
     sens,
     halo_x,
     halo_y,
     pack_y,
     put,
-    got,
     put_slot,
-    got_slot,
     in_sem,
-    out_sem,
     send_x,
     recv_x,
     send_y,
@@ -88,11 +96,14 @@
     gy = lax.axis_index("gy")
     me = gx * size_y + gy
 
+    got, got_slot = put_out, slot_out
+    elec = [elec_steps.at[step] for step in range(STEPS)] + [last_elec]
+
     loads = [
         pltpu.make_async_copy(source, target, in_sem.at[place])
         for place, (source, target) in enumerate(
             [
-                (e_in, elec),
+                (e_in, elec[0]),
                 (h_in, magn),
                 (mat_in, mat),
                 (kid_in, kid),
@@ -135,22 +146,24 @@
     def z_down(v):
         return jnp.where(col_z == 0, 0.0, pltpu.roll(v, 1, 1))
 
-    def h_plane(x, last):
-        ex, ey, ez = elec[0, x], elec[1, x], elec[2, x]
-        dx_ey = -ey if last else elec[1, x + 1] - ey
-        dx_ez = -ez if last else elec[2, x + 1] - ez
+    def h_plane(step, x, last):
+        elec_now = elec[step]
+        ex, ey, ez = elec_now[0, x], elec_now[1, x], elec_now[2, x]
+        dx_ey = -ey if last else elec_now[1, x + 1] - ey
+        dx_ez = -ez if last else elec_now[2, x + 1] - ez
         magn[0, x] = magn[0, x] - COURANT * ((y_up(ez) - ez) - (z_up(ey) - ey))
         magn[1, x] = magn[1, x] - COURANT * ((z_up(ex) - ex) - dx_ez)
         magn[2, x] = magn[2, x] - COURANT * (dx_ey - (y_up(ex) - ex))
 
-    def e_plane(x, first):
+    def e_plane(step, x, first):
+        elec_now, elec_new = elec[step], elec[step + 1]
         hx, hy, hz = magn[0, x], magn[1, x], magn[2, x]
         dx_hy = hy if first else hy - magn[1, x - 1]
         dx_hz = hz if first else hz - magn[2, x - 1]
         factor = scale[x]
-        elec[0, x] = elec[0, x] + factor * ((hz - y_down(hz)) - (hy - z_down(hy)))
-        elec[1, x] = elec[1, x] + factor * ((hx - z_down(hx)) - dx_hz)
-        elec[2, x] = elec[2, x] + factor * (dx_hy - (hx - y_down(hx)))
+        elec_new[0, x] = elec_now[0, x] + factor * ((hz - y_down(hz)) - (hy - z_down(hy)))
+        elec_new[1, x] = elec_now[1, x] + factor * ((hx - z_down(hx)) - dx_hz)
+        elec_new[2, x] = elec_now[2, x] + factor * (dx_hy - (hx - y_down(hx)))
 
     def loop(low, high, body):
         def run(x, carry):
@@ -159,13 +172,13 @@
 
         lax.fori_loop(low, high, run, 0)
 
-    def h_interior():
-        loop(0, cells_x - 1, lambda x: h_plane(x, False))
-        h_plane(cells_x - 1, True)
-
-    def e_interior():
-        e_plane(0, True)
-        loop(1, cells_x, lambda x: e_plane(x, False))
+    def h_interior(step):
+        loop(0, cells_x - 1, lambda x: h_plane(step, x, False))
+        h_plane(step, cells_x - 1, True)
+
+    def e_interior(step):
+        e_plane(step, 0, True)
+        loop(1, cells_x, lambda x: e_plane(step, x, False))
 
     def x_copy(half, source, shift):
         return pltpu.make_async_remote_copy(
@@ -193,7 +206,7 @@
     def copies(half):
         if half % 2 == 0:
             return (
-                (has_before_x, has_after_x, x_copy(half, elec.at[pl.ds(1, 2), 0], -1)),
+                (has_before_x, has_after_x, x_copy(half, elec[half // 2].at[pl.ds(1, 2), 0], -1)),
                 (has_before_y, has_after_y, y_copy(half, -1)),
             )
         return (
@@ -208,7 +221,7 @@
         def _():
             over_x.start()
 
-        field, row = (elec, 0) if half % 2 == 0 else (magn, cells_y - 1)
+        field, row = (elec[half // 2], 0) if half % 2 == 0 else (magn, cells_y - 1)
         pack_y[half, 0] = field[0, :, pl.ds(row, 1), :]
         pack_y[half, 1] = field[2, :, pl.ds(row, 1), :]
 
@@ -218,6 +231,7 @@
 
     def receive(half):
         (to_x, from_x, over_x), (to_y, from_y, over_y) = copies(half)
+        elec_new = elec[half // 2 + 1]
 
         @pl.when(from_y)
         def _():
@@ -229,8 +243,8 @@
             else:
                 row = pl.ds(0, 1)
                 factor = scale[:, row, :]
-                elec[0, :, row, :] = elec[0, :, row, :] - factor * halo_y[half, 1]
-                elec[2, :, row, :] = elec[2, :, row, :] + factor * halo_y[half, 0]
+                elec_new[0, :, row, :] = elec_new[0, :, row, :] - factor * halo_y[half, 1]
+                elec_new[2, :, row, :] = elec_new[2, :, row, :] + factor * halo_y[half, 0]
 
         @pl.when(from_x)
         def _():
@@ -241,8 +255,8 @@
                 magn[2, last] = magn[2, last] - COURANT * halo_x[half, 0]
             else:
                 factor = scale[0]
-                elec[1, 0] = elec[1, 0] + factor * halo_x[half, 1]
-                elec[2, 0] = elec[2, 0] - factor * halo_x[half, 0]
+                elec_new[1, 0] = elec_new[1, 0] + factor * halo_x[half, 1]
+                elec_new[2, 0] = elec_new[2, 0] - factor * halo_x[half, 0]
 
         @pl.when(to_x)
         def _():
@@ -276,28 +290,33 @@
         table = jnp.concatenate(
             [jnp.where(own, values[step : step + 1], 0.0) for step in range(STEPS)], axis=0
         )
-        return jnp.concatenate(split2(table), axis=0)
+        coefs[...] = jnp.concatenate(split2(table), axis=0)
 
     def make_weights(low, high):
-        coefs = make_coefs()
         half = STEPS * cells_y
 
         def plane(index):
-            comp, x = index // cells_x, lax.rem(index, cells_x)
+            comp, x = lax.rem(index, 3), index // 3
             block = dft[:, :, comp, x].reshape(2 * waves * cells_y, depth)
-            both = dot(coefs, block)
+            both = dot(coefs[...], block)
             weights[:, comp, x] = (both[:half] + both[half:]).reshape(STEPS, cells_y, depth)
 
-        loop(low * cells_x, high * cells_x, plane)
-
-    def add_sens(step):
+        def several(index):
+            for extra in range(UNROLL):
+                plane(index * UNROLL + extra)
+
+        loop(low, high, several)
+
+    def add_sens(low, high):
         def plane(x):
-            total = elec[0, x] * weights[step, 0, x]
-            total = total + elec[1, x] * weights[step, 1, x]
-            total = total + elec[2, x] * weights[step, 2, x]
+            total = None
+            for step in range(low, high):
+                for comp in range(3):
+                    term = elec[step + 1][comp, x] * weights[step, comp, x]
+                    total = term if total is None else total + term
             for block in range(depth // 128):
                 lanes = total[:, block * 128 : (block + 1) * 128]
-                sens[block, x] = lanes if step == 0 else sens[block, x] + lanes
+                sens[block, x] = lanes if low == 0 else sens[block, x] + lanes
 
         loop(0, cells_x, plane)
 
@@ -306,14 +325,6 @@
         spread = dot(pick, values.astype(F32).astype(BF16))
         keep = iota((tiles, tile_y), 1) == lax.rem(iota((tiles, tile_y), 0), tile_y)
         return jnp.sum(jnp.where(keep, spread, 0.0), axis=1, keepdims=True)
-
-    def as_row(values):
-        rows, lanes = values.shape
-        size = rows * lanes
-        pick = (iota((rows, size), 1) // lanes == iota((rows, size), 0)).astype(BF16)
-        spread = dot_rows(values.astype(F32).astype(BF16), pick)
-        keep = iota((lanes, size), 0) == lax.rem(iota((lanes, size), 1), lanes)
-        return jnp.sum(jnp.where(keep, spread, 0.0), axis=0, keepdims=True)
 
     def positions():
         own_row = as_row(owner[...])
@@ -358,53 +369,56 @@
             kern_high[:, index * voxels : (index + 1) * voxels] = high
             kern_low[:, index * voxels : (index + 1) * voxels] = low
 
+    units = 3 * cells_x // UNROLL
+
+    def share(part):
+        make_weights(units * part // 5, units * (part + 1) // 5)
+
     loads[0].wait()
     pl.semaphore_wait(barrier, count - 1)
     send(0)
     loads[1].wait()
-    h_interior()
+    h_interior(0)
     loads[2].wait()
     make_scale()
+    make_coefs()
     receive(0)
     send(1)
-    e_interior()
+    e_interior(0)
     loads[7].wait()
-    make_weights(0, 2)
+    share(0)
     receive(1)
     send(2)
-    h_interior()
-    make_weights(2, 3)
-    add_sens(0)
-    receive(2)
-    send(3)
-    e_interior()
+    h_interior(1)
     for place in (3, 4, 5):
         loads[place].wait()
     send_slots()
+    receive(2)
+    send(3)
+    e_interior(1)
+    share(1)
     receive(3)
     send(4)
-    h_interior()
-    add_sens(1)
+    h_interior(2)
+    share(2)
     receive(4)
     send(5)
-    e_interior()
+    e_interior(2)
+    share(3)
+    receive(5)
+    send(6)
+    h_interior(3)
+    share(4)
+    receive(6)
+    send(7)
+    e_interior(3)
     loads[6].wait()
     make_kernels()
-    receive(5)
-    send(6)
-    h_interior()
-    add_sens(2)
-    receive(6)
-    send(7)
-    store_h = pltpu.make_async_copy(magn, h_out, out_sem.at[0])
-    store_h.start()
-    e_interior()
+    add_sens(0, STEPS - 1)
     wait_all(put_slot, 0)
     wait_all(got_slot, 1)
     receive(7)
-    store_e = pltpu.make_async_copy(elec, e_out, out_sem.at[1])
-    store_e.start()
-    add_sens(3)
+    add_sens(STEPS - 1, STEPS)
 
     total = jnp.zeros((tiles, kernels * voxels), F32)
     for a in range(2):
@@ -445,16 +459,26 @@
         return carry
 
     lax.fori_loop(1, count, push, 0)
+    wait_all(got, 3)
+    wait_all(put, 2)
+
+
+def finish(capacity, elec, magn, got, got_slot, e_out, h_out, grad_ref, sems):
+    stores = [
+        pltpu.make_async_copy(elec, e_out, sems.at[0]),
+        pltpu.make_async_copy(magn, h_out, sems.at[1]),
+    ]
+    for store in stores:
+        store.start()
+    count, _, voxels = got.shape
     received = got_slot[...].reshape(count, 128)[:, :capacity]
     gather = (
         iota((SLOTS, count * capacity), 0).astype(F32) == as_row(received)
     ).astype(BF16)
-    wait_all(got, 3)
     high, low = split2(got[...].reshape(count * capacity, voxels))
     grad_ref[...] = dot(gather, high) + dot(gather, low)
-    wait_all(put, 2)
-    store_h.wait()
-    store_e.wait()
+    for store in stores:
+        store.wait()
 
 
 def per_device(
@@ -477,16 +501,21 @@
     tiles = cells_x * cells_y // 4
     capacity = max(2, (2 * tiles + count - 1) // count)
     field = jax.ShapeDtypeStruct(e_field.shape, F32)
-    anywhere = pl.BlockSpec(memory_space=pl.ANY)
+    anywhere = pl.BlockSpec(memory_space=pltpu.HBM)
     halves = 2 * STEPS
-    return pl.pallas_call(
+    here = pl.BlockSpec(memory_space=pltpu.VMEM)
+    state = pl.pallas_call(
         functools.partial(kernel, size_x, size_y, capacity),
-        out_shape=(field, field, jax.ShapeDtypeStruct((SLOTS, voxels), F32)),
-        in_specs=[pl.BlockSpec(memory_space=pltpu.SMEM)] * 2 + [anywhere] * 8,
-        out_specs=(anywhere, anywhere, pl.BlockSpec(memory_space=pltpu.VMEM)),
-        scratch_shapes=[
+        out_shape=(
             pltpu.VMEM(e_field.shape, F32),
             pltpu.VMEM(h_field.shape, F32),
+            pltpu.VMEM((count, capacity, voxels), F32),
+            pltpu.VMEM((count, 1, 128), F32),
+        ),
+        in_specs=[pl.BlockSpec(memory_space=pltpu.SMEM)] * 2 + [anywhere] * 8,
+        out_specs=(here,) * 4,
+        scratch_shapes=[
+            pltpu.VMEM((STEPS,) + e_field.shape, F32),
             pltpu.VMEM(material.shape, jnp.int32),
             pltpu.VMEM(material.shape, F32),
             pltpu.VMEM(forward_dft.shape, BF16),
@@ -496,17 +525,15 @@
             pltpu.VMEM(kernel_id.shape, jnp.int32),
             pltpu.VMEM(owner_map.shape, jnp.int32),
             pltpu.VMEM(slot_map.shape, jnp.int32),
+            pltpu.VMEM((2 * STEPS * cells_y, 2 * forward_dft.shape[0] * cells_y), BF16),
             pltpu.VMEM((STEPS,) + e_field.shape, F32),
             pltpu.VMEM((depth // 128, cells_x, cells_y, 128), F32),
             pltpu.VMEM((halves, 2, cells_y, depth), F32),
             pltpu.VMEM((halves, 2, cells_x, 1, depth), F32),
             pltpu.VMEM((halves, 2, cells_x, 1, depth), F32),
             pltpu.VMEM((count, capacity, voxels), F32),
-            pltpu.VMEM((count, capacity, voxels), F32),
-            pltpu.VMEM((count, 1, 128), F32),
             pltpu.VMEM((count, 1, 128), F32),
             pltpu.SemaphoreType.DMA((8,)),
-            pltpu.SemaphoreType.DMA((2,)),
             pltpu.SemaphoreType.DMA((halves,)),
             pltpu.SemaphoreType.DMA((halves,)),
             pltpu.SemaphoreType.DMA((halves,)),
@@ -528,6 +555,16 @@
         owner_map,
         slot_map,
     )
+    return pl.pallas_call(
+        functools.partial(finish, capacity),
+        out_shape=(field, field, jax.ShapeDtypeStruct((SLOTS, voxels), F32)),
+        in_specs=[here] * 4,
+        out_specs=(anywhere, anywhere, here),
+        scratch_shapes=[pltpu.SemaphoreType.DMA((2,))],
+        compiler_params=pltpu.CompilerParams(
+            has_side_effects=True, vmem_limit_bytes=8 * 2**20
+        ),
+    )(*[pltpu.with_memory_space_constraint(part, pltpu.VMEM) for part in state])
 
 
 def solution(mesh):

time: 54.2 us -> 46.2 us (0.85)
  local copies, waits for them, and re-layouts: 4.61 us -> 0 us
  Pallas kernels: 48.7 us -> 45.3 us
    pallas_call x1, Pallas kernels: 48.7 us -> 43 us  [per_device(): pl.pallas_call(functools.partial(kernel, size_x, size_y, capacity), out_s...]
    unnamed x7 -> x0, local copies, waits for them, and re-layouts: 4.61 us -> none
    pallas_call x0 -> x1, Pallas kernels: none -> 2.3 us  [per_device(): pl.pallas_call(functools.partial(finish, capacity), out_shape=(field, fie...]
where the time goes in v2:
time: 46.2 us; the launch traced here: 46 us
  Pallas kernels  45.3 us (98%)
  between operations  0.64 us (1%)
    pallas_call x1, Pallas kernels, per_device(): pl.pallas_call(functools.partial(kernel, size_x, size_y, capacity), out_s...  43 us
    pallas_call x1, Pallas kernels, per_device(): pl.pallas_call(functools.partial(finish, capacity), out_shape=(field, fie...  2.3 us

profile of v2, /device:TPU:0, one launch (start us, length us, event | category | flops | bytes accessed | tf_op | source)
XLA Modules:
  0.0 46.0 jit_solution(2790717285543880882)
XLA Ops:
  0.6 43.0 %shard_map.121 = (f32[3,16,32,256]{3,2,1,0:T(8,128)S(1)}, f32[3,16,32,256]{3,2,1,0:T(8,128)S(1)}, f32[32,8,128]{2,1,0:T(8,128)S(1)}, f32[32,1,128]{2,1,0:T(1,128)S(1)}) custom-call(f32[8]{0:T(128)} %eps_ref.1, f32[4]{0:T(128)} %phase_ref.1, f32[3,16,32,256]{3,2,1,0:T(8,128)} %e_in.1, f32[3,16,32,256]{3,2,1,0:T(8,128)} %h_in.1, s32[16,32,256]{2,1,0:T(8,128)} %mat_in.1, ...), custom_call_target="tpu_custom_call" | custom-call | tf_op jit(solution)/shard_map/pallas_call | solution.py:507
  43.7 2.3 %shard_map.122 = (f32[3,16,32,256]{3,2,1,0:T(8,128)}, f32[3,16,32,256]{3,2,1,0:T(8,128)}, f32[64,128]{1,0:T(8,128)}) custom-call(f32[3,16,32,256]{3,2,1,0:T(8,128)S(1)} %get-tuple-element.7.elec, f32[3,16,32,256]{3,2,1,0:T(8,128)S(1)} %get-tuple-element.8.magn, f32[32,8,128]{2,1,0:T(8,128)S(1)} %get-tuple-element.9.got, ...), custom_call_target="tpu_custom_call" | custom-call | tf_op jit(solution)/shard_map/pallas_call | solution.py:558
